TPU v7x, 32 devices: a whole 2x2x4 slice. The times are simulated.
32 devices in a mesh: dp: 8 (over z, y), upd: 4 (over x, core).
Axes of the slice: x: 2, y: 2, z: 4, core: 2. Of those that a mesh axis runs over, the one named last changes fastest.
Arguments:
- inputs: bfloat16 [256, 128, 768], P(('dp', 'upd')), may hold values from -6 to 6
- memory: bfloat16 [256, 256, 768], P(('dp', 'upd')), may hold values from -6 to 6
- cotangent: bfloat16 [256, 128, 768], P(('dp', 'upd')), may hold values from -6 to 6
- lengths: int32 [256], P(('dp', 'upd')), may hold values from 1 to 128, as said below
- memory_len: int32 [256], P(('dp', 'upd')), may hold values from 64 to 225, as said below
- square_master: float32 [8, 768, 768], P(None, ('dp', 'upd')), may hold values from -0.21875 to 0.21875
- tall_master: float32 [2, 3072, 768], P(None, ('dp', 'upd'))
- square_momentum: float32 [8, 768, 768], P(None, ('dp', 'upd'))
- tall_momentum: float32 [2, 3072, 768], P(None, ('dp', 'upd'))
- vectors: bfloat16 [17, 768], replicated, may hold values from -1.5 to 1.5
- feed_vectors: bfloat16 [3, 3072], replicated, may hold values from -1.5 to 1.5
- head_scale: bfloat16 [12], replicated, may hold values from 0.25 to 1.75
- relative: bfloat16 [12, 128], replicated, may hold values from -4 to 4
Outputs:
- output: bfloat16 [256, 128, 768], P(('dp', 'upd'))
- input_gradient: bfloat16 [256, 128, 768], P(('dp', 'upd'))
- memory_gradient: bfloat16 [256, 256, 768], P(('dp', 'upd'))
- square_state: float32 [8, 768, 768], P(None, ('dp', 'upd'))
- tall_state: float32 [2, 3072, 768], P(None, ('dp', 'upd'))
- square_weight: float32 [8, 768, 768], P(None, ('dp', 'upd'))
- tall_weight: float32 [2, 3072, 768], P(None, ('dp', 'upd'))
- vector_gradient: float32 [17, 768], P(None, ('dp', 'upd'))
- feed_gradient: float32 [3, 3072], P(None, ('dp', 'upd'))
- scale_gradient: float32 [12], replicated
- bias_gradient: float32 [12, 128], replicated
Inputs may be any that keep to these rules, and one draw needn't show every extreme that they name: `lengths`: positions at or past an item's count are padding; some item has exactly 128. `memory_len`: each item has 64 or 225 real memory rows, the first ones; both occur.
All inputs are finite; a program needn't handle non-finite values.
Results may differ from a plain program's by a relative error of at most 0.02.
Values may be sent and summed in bfloat16 or wider, within the bound.
A program may use at most 384 MiB of HBM per device.

v0:
```python
import jax
import jax.numpy as jnp
from jax import lax
from jax.sharding import PartitionSpec as P

D = 768
FF = 3072
ITERS = 5
NORM_EPSILON = 1e-05
FLOOR_EPSILON = 1e-07
FIRST_TERM = 3.4445
SECOND_TERM = -4.775
THIRD_TERM = 2.0315
MOMENTUM_DECAY = 0.95
LEARN_RATE = 0.8
WEIGHT_DECAY = 0.01
NEGATIVE_LARGE = -1e30


def plain_round(values):
    return lax.optimization_barrier(values.astype(jnp.bfloat16)).astype(jnp.float32)


def same_value(values):
    return values


def value_keep(values):
    return (plain_round(values), None)


def value_pass(kept, slope):
    return (slope,)


def gradient_keep(values):
    return (values, None)


def gradient_round(kept, slope):
    return (plain_round(slope),)


def round_value(values):
    wrapped = jax.custom_vjp(plain_round)
    wrapped.defvjp(value_keep, value_pass)
    return wrapped(values)


def round_gradient(values):
    wrapped = jax.custom_vjp(same_value)
    wrapped.defvjp(gradient_keep, gradient_round)
    return wrapped(values)


def norm_rows(values, gain, shift):
    center = values - jnp.mean(values, axis=-1, keepdims=True)
    spread = jnp.mean(center * center, axis=-1, keepdims=True)
    return center * lax.rsqrt(spread + NORM_EPSILON) * gain + shift


def attend(query, keys, values, allowed, bias):
    scores = jnp.einsum("bqhe,bkhe->bhqk", query, keys) + bias
    scores = jnp.where(allowed, round_gradient(scores), NEGATIVE_LARGE)
    weights = jnp.exp(scores - jnp.max(scores, axis=-1, keepdims=True))
    weights = round_value(weights / jnp.sum(weights, axis=-1, keepdims=True))
    return round_gradient(jnp.einsum("bhqk,bkhe->bqhe", weights, values))


def split_heads(values, head_count):
    return values.reshape(
        values.shape[0], values.shape[1], head_count, values.shape[2] // head_count
    )


def layer_block(
    inputs, memory, memory_len, square, tall, vectors, feed_vectors, head_scale, relative
):
    item_count, query_count, model_width = inputs.shape
    head_count = head_scale.shape[0]
    memory_slots = memory.shape[1]
    normed = round_value(norm_rows(inputs, vectors[0], vectors[1]))
    query = round_gradient(round_value((jnp.matmul(normed, square[0]) + vectors[2]) * 0.125))
    keys = round_gradient(round_value(jnp.matmul(normed, square[1])))
    values = round_gradient(round_value(jnp.matmul(normed, square[2]) + vectors[3]))
    query_index = jnp.arange(query_count)[:, None]
    key_index = jnp.arange(query_count)[None, :]
    distance = jnp.clip(query_index - key_index, 0, query_count - 1)
    position_table = (distance[:, :, None] == jnp.arange(query_count)[None, None, :]).astype(
        jnp.float32
    )
    bias = jnp.einsum("hd,qkd->hqk", relative, position_table)[None]
    mixed = attend(
        split_heads(query, head_count),
        split_heads(keys, head_count),
        split_heads(values, head_count),
        (query_index >= key_index)[None, None],
        bias,
    )
    mixed = (mixed * head_scale[None, None, :, None]).reshape(item_count, query_count, model_width)
    mixed = round_value(norm_rows(mixed, vectors[5], vectors[6]))
    hidden = inputs + round_gradient(jnp.matmul(mixed, square[3]) + vectors[4])
    normed = round_value(norm_rows(hidden, vectors[7], vectors[8]))
    query = round_gradient(round_value((jnp.matmul(normed, square[4]) + vectors[9]) * 0.125))
    keys = round_gradient(round_value(jnp.matmul(memory, square[5])))
    values = round_gradient(round_value(jnp.matmul(memory, square[6]) + vectors[10]))
    allowed = (jnp.arange(memory_slots)[None, :] < memory_len[:, None])[:, None, None, :]
    mixed = attend(
        split_heads(query, head_count),
        split_heads(keys, head_count),
        split_heads(values, head_count),
        allowed,
        0.0,
    )
    mixed = round_value(
        norm_rows(mixed.reshape(item_count, query_count, model_width), vectors[12], vectors[13])
    )
    hidden = hidden + round_gradient(jnp.matmul(mixed, square[7]) + vectors[11])
    normed = round_value(norm_rows(hidden, vectors[14], vectors[15]))
    inner = round_gradient(jnp.matmul(normed, tall[0].T) + feed_vectors[0])
    active = round_value(
        norm_rows(jax.nn.gelu(inner, approximate=False), feed_vectors[1], feed_vectors[2])
    )
    return hidden + round_gradient(jnp.matmul(active, tall[1]) + vectors[16])


def gram_of(block):
    return jnp.einsum("wrd,wre->wde", block, block, precision=lax.Precision.HIGHEST)


def advance(current, gram):
    mixed = jnp.einsum("wrd,wde->wre", current, gram, precision=lax.Precision.HIGHEST)
    second = jnp.einsum("wrd,wde->wre", mixed, gram, precision=lax.Precision.HIGHEST)
    return FIRST_TERM * current + SECOND_TERM * mixed + THIRD_TERM * second


def both_grams(square, tall):
    joined = jnp.concatenate([gram_of(square), gram_of(tall)], axis=0)
    summed = lax.all_gather(
        lax.psum_scatter(joined, ("dp", "upd"), scatter_dimension=1, tiled=True).astype(
            jnp.bfloat16
        ),
        ("dp", "upd"),
        axis=1,
        tiled=True,
    ).astype(jnp.float32)
    return (summed[:8], summed[8:])


def shared_rows(square_state, tall_state):
    square_squares, tall_squares = lax.psum(
        (
            jnp.sum(square_state * square_state, axis=(1, 2)),
            jnp.sum(tall_state * tall_state, axis=(1, 2)),
        ),
        ("dp", "upd"),
    )
    square = square_state * (1.0 / (jnp.sqrt(square_squares) + FLOOR_EPSILON))[:, None, None]
    tall = tall_state * (1.0 / (jnp.sqrt(tall_squares) + FLOOR_EPSILON))[:, None, None]
    first_sweep = 0
    for sweep in range(first_sweep, ITERS):
        square_gram, tall_gram = both_grams(square, tall)
        square = advance(square, square_gram)
        tall = advance(tall, tall_gram)
    return (square, tall)


def local(
    inputs,
    memory,
    cotangent,
    lengths,
    memory_len,
    square_master,
    tall_master,
    square_momentum,
    tall_momentum,
    vectors,
    feed_vectors,
    head_scale,
    relative,
):
    square_copy, tall_copy = (
        lax.all_gather(square_master.astype(jnp.bfloat16), ("dp", "upd"), axis=1, tiled=True),
        lax.all_gather(tall_master.astype(jnp.bfloat16), ("dp", "upd"), axis=1, tiled=True),
    )
    params = (
        square_copy.astype(jnp.float32),
        tall_copy.astype(jnp.float32),
        vectors.astype(jnp.float32),
        feed_vectors.astype(jnp.float32),
        head_scale.astype(jnp.float32),
        relative.astype(jnp.float32),
    )

    def forward(params, inputs_full, memory_full):
        return layer_block(inputs_full, memory_full, memory_len, *params)

    output, pullback = jax.vjp(
        forward, params, inputs.astype(jnp.float32), memory.astype(jnp.float32)
    )
    valid = (jnp.arange(inputs.shape[1])[None, :] < lengths[:, None]).astype(jnp.float32)
    param_slopes, input_slope, memory_slope = pullback(
        cotangent.astype(jnp.float32) * valid[:, :, None]
    )
    square_slope, tall_slope, vector_slope, feed_slope, scale_slope, bias_slope = param_slopes
    total, scale_sum, bias_sum = lax.psum(
        (jnp.sum(lengths).astype(jnp.float32), scale_slope, bias_slope), ("dp", "upd")
    )
    square_sum, tall_sum, vector_sum, feed_sum = (
        lax.psum_scatter(square_slope, ("dp", "upd"), scatter_dimension=1, tiled=True),
        lax.psum_scatter(tall_slope, ("dp", "upd"), scatter_dimension=1, tiled=True),
        lax.psum_scatter(vector_slope, ("dp", "upd"), scatter_dimension=1, tiled=True),
        lax.psum_scatter(feed_slope, ("dp", "upd"), scatter_dimension=1, tiled=True),
    )
    factor = inputs.shape[0] * lax.axis_size("dp") * lax.axis_size("upd") / total
    square_state = MOMENTUM_DECAY * square_momentum + factor * square_sum
    tall_state = MOMENTUM_DECAY * tall_momentum + factor * tall_sum
    square, tall = shared_rows(square_state, tall_state)
    square_weight = square_master * (1.0 - LEARN_RATE * WEIGHT_DECAY) - LEARN_RATE * square
    tall_weight = (
        tall_master * (1.0 - LEARN_RATE * WEIGHT_DECAY)
        - LEARN_RATE * max(1.0, FF / D) ** 0.5 * tall
    )
    return (
        output.astype(jnp.bfloat16),
        input_slope.astype(jnp.bfloat16),
        memory_slope.astype(jnp.bfloat16),
        square_state,
        tall_state,
        square_weight,
        tall_weight,
        factor * vector_sum,
        factor * feed_sum,
        factor * scale_sum,
        factor * bias_sum,
    )


def solution(mesh):
    placed = (
        P(("dp", "upd"), None, None),
        P(("dp", "upd"), None, None),
        P(("dp", "upd"), None, None),
        P(("dp", "upd")),
        P(("dp", "upd")),
        P(None, ("dp", "upd"), None),
        P(None, ("dp", "upd"), None),
        P(None, ("dp", "upd"), None),
        P(None, ("dp", "upd"), None),
        P(),
        P(),
        P(),
        P(),
    )
    return jax.shard_map(
        local,
        mesh=mesh,
        in_specs=placed,
        out_specs=(
            P(("dp", "upd"), None, None),
            P(("dp", "upd"), None, None),
            P(("dp", "upd"), None, None),
            P(None, ("dp", "upd"), None),
            P(None, ("dp", "upd"), None),
            P(None, ("dp", "upd"), None),
            P(None, ("dp", "upd"), None),
            P(None, ("dp", "upd")),
            P(None, ("dp", "upd")),
            P(),
            P(),
        ),
        check_vma=False,
    )
```

profile of v0, /device:TPU:0, one launch (start us, length us, event | category | flops | bytes accessed | tf_op | source)
XLA Modules:
  0.0 2761.8 jit_solution(14452595280854810627)
XLA Ops:
  28.9 67.6 %all-gather.8.cloned.1.call-done = bf16[8,768,768]{2,1,0:T(8,128)(2,1)} async-done(((bf16[8,24,768]{2,1,0:T(8,128)(2,1)}), bf16[8,768,768]{2,1,0:T(8,128)(2,1)}) %all-gather.8.cloned.1.call-update) | async-done | bytes 9437200 | tf_op jit(solution)/shard_map/all_gather | solution.py:184
  212.7 13.1 fusion.59
  225.8 35.1 %fusion.208 = (f32[8,128]{1,0:T(8,128)S(1)}, f32[8,128,3072]{2,1,0:T(8,128)S(1)}, f32[8,128,3072]{2,1,0:T(8,128)}) fusion(f32[8,128,3072]{2,1,0:T(8,128)} %get-tuple-element.100, f32[3072]{0:T(1024)S(1)} %bitcast.312, u8[128,3072]{1,0:T(8,128)(4,1)S(1)} %get-tuple-element.14, u8[128,3072]{1,0:T(8,128)(4,1)S(1)} %get-tuple-element.13), kind=kLoop, calls=%fused_computation.340 | loop fusion | flops 223345664 | bytes 38551552 | tf_op jit(solution)/shard_map/jvp()/reduce_sum | solution.py:57
  281.2 19.7 add_convert_fusion
  351.3 12.2 multiply_reduce_fusion.1
  473.3 42.2 %psum.35 = f32[]{:T(128)} all-reduce(f32[]{:T(128)S(6)} %convert_element_type.296), channel_id=1, replica_groups=mesh['dp'=8,'upd'=4] {'dp','upd'}, use_global_device_ids=true, to_apply=%region_35.36 | all-reduce | flops 1 | bytes 8 | tf_op jit(solution)/shard_map/psum | solution.py:207
  549.2 200.3 %reduce-scatter.12.cloned.1.call-done = f32[8,24,768]{2,1,0:T(8,128)} async-done(((f32[8,768,768]{2,1,0:T(8,128)}), f32[8,24,768]{2,1,0:T(8,128)}) %reduce-scatter.12.cloned.1.call-update) | async-done | bytes 589840 | tf_op jit(solution)/shard_map/reduce_scatter | solution.py:211
  750.7 40.5 %all-reduce.31 = (f32[2]{0:T(128)S(1)}, f32[8]{0:T(128)S(1)}, f32[17,768]{1,0:T(8,128)}, f32[12]{0:T(128)}, f32[12,128]{1,0:T(8,128)}) all-reduce(f32[2]{0:T(128)S(1)} %get-tuple-element.61, f32[8]{0:T(128)S(1)} %get-tuple-element.59, f32[17,768]{1,0:T(8,128)S(1)} %pad_add_fusion.2, ...), channel_id=1, replica_groups=mesh['dp'=8,'upd'=4] {'dp','upd'}, use_global_device_ids=true, to_apply=%region_41.42 | all-reduce | flops 14614 | bytes 116912 | tf_op jit(solution)/shard_map/psum | solution.py:151
  791.2 15.9 fusion.177
  819.6 231.2 %reduce-scatter.16.cloned.1.call-done = f32[10,24,768]{2,1,0:T(8,128)} async-done(((f32[10,768,768]{2,1,0:T(8,128)}), f32[10,24,768]{2,1,0:T(8,128)}) %reduce-scatter.16.cloned.1.call-update) | async-done | bytes 737296 | tf_op jit(solution)/shard_map/reduce_scatter | solution.py:140
  1052.7 93.8 %all-gather.12.cloned.1.call-done = bf16[10,768,768]{2,1,0:T(8,128)(2,1)} async-done(((bf16[10,24,768]{2,1,0:T(8,128)(2,1)}), bf16[10,768,768]{2,1,0:T(8,128)(2,1)}) %all-gather.12.cloned.1.call-update) | async-done | bytes 11796496 | tf_op jit(solution)/shard_map/all_gather | solution.py:139
  1159.6 15.6 fusion.214
  1193.5 229.9 %reduce-scatter.18.cloned.1.call-done = f32[10,24,768]{2,1,0:T(8,128)} async-done(((f32[10,768,768]{2,1,0:T(8,128)}), f32[10,24,768]{2,1,0:T(8,128)}) %reduce-scatter.18.cloned.1.call-update) | async-done | bytes 737296 | tf_op jit(solution)/shard_map/reduce_scatter | solution.py:140
  1425.3 93.5 %all-gather.14.cloned.1.call-done = bf16[10,768,768]{2,1,0:T(8,128)(2,1)} async-done(((bf16[10,24,768]{2,1,0:T(8,128)(2,1)}), bf16[10,768,768]{2,1,0:T(8,128)(2,1)}) %all-gather.14.cloned.1.call-update) | async-done | bytes 11796496 | tf_op jit(solution)/shard_map/all_gather | solution.py:139
  1531.8 15.6 fusion.216
  1565.5 229.9 %reduce-scatter.20.cloned.1.call-done = f32[10,24,768]{2,1,0:T(8,128)} async-done(((f32[10,768,768]{2,1,0:T(8,128)}), f32[10,24,768]{2,1,0:T(8,128)}) %reduce-scatter.20.cloned.1.call-update) | async-done | bytes 737296 | tf_op jit(solution)/shard_map/reduce_scatter | solution.py:140
  1797.4 93.8 %all-gather.16.cloned.1.call-done = bf16[10,768,768]{2,1,0:T(8,128)(2,1)} async-done(((bf16[10,24,768]{2,1,0:T(8,128)(2,1)}), bf16[10,768,768]{2,1,0:T(8,128)(2,1)}) %all-gather.16.cloned.1.call-update) | async-done | bytes 11796496 | tf_op jit(solution)/shard_map/all_gather | solution.py:139
  1904.2 15.6 fusion.218
  1937.9 229.9 %reduce-scatter.22.cloned.1.call-done = f32[10,24,768]{2,1,0:T(8,128)} async-done(((f32[10,768,768]{2,1,0:T(8,128)}), f32[10,24,768]{2,1,0:T(8,128)}) %reduce-scatter.22.cloned.1.call-update) | async-done | bytes 737296 | tf_op jit(solution)/shard_map/reduce_scatter | solution.py:140
  2169.8 93.4 %all-gather.18.cloned.1.call-done = bf16[10,768,768]{2,1,0:T(8,128)(2,1)} async-done(((bf16[10,24,768]{2,1,0:T(8,128)(2,1)}), bf16[10,768,768]{2,1,0:T(8,128)(2,1)}) %all-gather.18.cloned.1.call-update) | async-done | bytes 11796496 | tf_op jit(solution)/shard_map/all_gather | solution.py:139
  2276.2 15.6 fusion.220
  2315.5 224.5 %reduce-scatter.24.cloned.1.call-done = f32[10,24,768]{2,1,0:T(8,128)} async-done(((f32[10,768,768]{2,1,0:T(8,128)}), f32[10,24,768]{2,1,0:T(8,128)}) %reduce-scatter.24.cloned.1.call-update) | async-done | bytes 737296 | tf_op jit(solution)/shard_map/reduce_scatter | solution.py:140
  2562.8 79.6 %reduce-scatter.26.cloned.1.call-done = f32[96,3]{1,0:T(8,128)} async-done(((f32[3072,3]{1,0:T(8,128)}), f32[96,3]{1,0:T(8,128)}) %reduce-scatter.26.cloned.1.call-update) | async-done | bytes 1168
  2646.3 90.7 %all-gather.20.cloned.1.call-done = bf16[10,768,768]{2,1,0:T(8,128)(2,1)} async-done(((bf16[10,24,768]{2,1,0:T(8,128)(2,1)}), bf16[10,768,768]{2,1,0:T(8,128)(2,1)}) %all-gather.20.cloned.1.call-update) | async-done | bytes 11796496 | tf_op jit(solution)/shard_map/all_gather | solution.py:139
  (520 shorter events, 545.1 us)
Async XLA Ops:
  7.2 89.2 %all-gather.8.cloned.1.call-start = ((), (), s32[]{:S(2)}) async-start(), calls=%async_computation.8 | async-start | bytes 9732096 | tf_op jit(solution)/shard_map/all_gather | solution.py:184
  9.2 203.5 %all-gather.10.cloned.1.call-start = ((), (), s32[]{:S(2)}) async-start(), calls=%async_computation.9 | async-start | bytes 9732096 | tf_op jit(solution)/shard_map/all_gather | solution.py:185
  11.1 536.8 %reduce-scatter.14.cloned.1.call-start = ((), (), s32[]{:S(2)}) async-start(), calls=%async_computation.11 | async-start | bytes 19464192 | tf_op jit(solution)/shard_map/reduce_scatter | solution.py:212
  333.8 415.6 %reduce-scatter.12.cloned.1.call-start = ((), (), s32[]{:S(2)}) async-start(), calls=%async_computation.10 | async-start | bytes 19464192 | tf_op jit(solution)/shard_map/reduce_scatter | solution.py:211
  471.4 579.4 %reduce-scatter.16.cloned.1.call-start = ((), (), s32[]{:S(2)}) async-start(), calls=%async_computation.12 | async-start | bytes 24330240 | tf_op jit(solution)/shard_map/reduce_scatter | solution.py:140
  540.6 208.9 %copy-start.77 = (f32[8,24,768]{2,1,0:T(8,128)S(1)}, f32[8,24,768]{2,1,0:T(8,128)}, u32[]{:S(2)}) copy-start(f32[8,24,768]{2,1,0:T(8,128)} %param.20) | copy-start | bytes 1769476
  549.2 629.0 %copy-start.42 = (f32[2,96,768]{2,1,0:T(8,128)}, f32[2,96,768]{2,1,0:T(8,128)S(1)}, u32[]{:S(2)}) copy-start(f32[2,96,768]{2,1,0:T(8,128)S(1)} %get-tuple-element.62) | copy-start | bytes 1769476
  750.7 402.2 %copy-start.41 = (f32[8,24,768]{2,1,0:T(8,128)}, f32[8,24,768]{2,1,0:T(8,128)S(1)}, u32[]{:S(2)}) copy-start(f32[8,24,768]{2,1,0:T(8,128)S(1)} %get-tuple-element.60) | copy-start | bytes 1769476
  819.6 327.0 %all-gather.12.cloned.1.call-start = ((), (), s32[]{:S(2)}) async-start(), calls=%async_computation.13 | async-start | bytes 12165120 | tf_op jit(solution)/shard_map/all_gather | solution.py:139
  1052.7 370.6 %reduce-scatter.18.cloned.1.call-start = ((), (), s32[]{:S(2)}) async-start(), calls=%async_computation.14 | async-start | bytes 24330240 | tf_op jit(solution)/shard_map/reduce_scatter | solution.py:140
  1193.4 325.4 %all-gather.14.cloned.1.call-start = ((), (), s32[]{:S(2)}) async-start(), calls=%async_computation.15 | async-start | bytes 12165120 | tf_op jit(solution)/shard_map/all_gather | solution.py:139
  1425.2 370.2 %reduce-scatter.20.cloned.1.call-start = ((), (), s32[]{:S(2)}) async-start(), calls=%async_computation.16 | async-start | bytes 24330240 | tf_op jit(solution)/shard_map/reduce_scatter | solution.py:140
  1565.5 325.7 %all-gather.16.cloned.1.call-start = ((), (), s32[]{:S(2)}) async-start(), calls=%async_computation.17 | async-start | bytes 12165120 | tf_op jit(solution)/shard_map/all_gather | solution.py:139
  1797.4 370.5 %reduce-scatter.22.cloned.1.call-start = ((), (), s32[]{:S(2)}) async-start(), calls=%async_computation.18 | async-start | bytes 24330240 | tf_op jit(solution)/shard_map/reduce_scatter | solution.py:140
  1937.9 325.3 %all-gather.18.cloned.1.call-start = ((), (), s32[]{:S(2)}) async-start(), calls=%async_computation.19 | async-start | bytes 12165120 | tf_op jit(solution)/shard_map/all_gather | solution.py:139
  2169.7 370.2 %reduce-scatter.24.cloned.1.call-start = ((), (), s32[]{:S(2)}) async-start(), calls=%async_computation.20 | async-start | bytes 24330240 | tf_op jit(solution)/shard_map/reduce_scatter | solution.py:140
  2309.9 332.4 %reduce-scatter.26.cloned.1.call-start = ((), (), s32[]{:S(2)}) async-start(), calls=%async_computation.22 | async-start | bytes 1622016
  2313.6 228.2 %copy-start.113 = (f32[8,128]{1,0:T(8,128)S(1)}, f32[8,128]{1,0:T(8,128)}, u32[]{:S(2)}) copy-start(f32[8,128]{1,0:T(8,128)} %get-tuple-element.27) | copy-start | bytes 12292
  2313.7 228.2 %copy-start.7 = (bf16[8,128,768]{2,1,0:T(8,128)(2,1)S(1)}, bf16[8,128,768]{2,1,0:T(8,128)(2,1)}, u32[]{:S(2)}) copy-start(bf16[8,128,768]{2,1,0:T(8,128)(2,1)} %param.13) | copy-start | bytes 4718596
  2313.7 228.2 %copy-start.81 = (f32[8,128]{1,0:T(8,128)S(1)}, f32[8,128]{1,0:T(8,128)}, u32[]{:S(2)}) copy-start(f32[8,128]{1,0:T(8,128)} %copy-done.79) | copy-start | bytes 12292
  2313.7 228.2 %copy-start.88 = (f32[768]{0:T(1024)S(1)}, f32[768]{0:T(1024)}, u32[]{:S(2)}) copy-start(f32[768]{0:T(1024)} %copy-done.86) | copy-start | bytes 9220
  2313.7 228.2 %copy-start.91 = (f32[8,128]{1,0:T(8,128)S(1)}, f32[8,128]{1,0:T(8,128)}, u32[]{:S(2)}) copy-start(f32[8,128]{1,0:T(8,128)} %copy-done.89) | copy-start | bytes 12292
  2313.7 228.2 %copy-start.106 = (f32[8,128]{1,0:T(8,128)S(1)}, f32[8,128]{1,0:T(8,128)}, u32[]{:S(2)}) copy-start(f32[8,128]{1,0:T(8,128)} %copy-done.105) | copy-start | bytes 12292
  2315.5 421.6 %all-gather.20.cloned.1.call-start = ((), (), s32[]{:S(2)}) async-start(), calls=%async_computation.21 | async-start | bytes 12165120 | tf_op jit(solution)/shard_map/all_gather | solution.py:139
  (131 other events, 1850.6 us)
Sparse Core Ops, SparseCore 0:
  11.5 84.8 all-gather.7
  99.9 80.6 all-gather.9
  333.9 205.2 reduce-scatter.13
  545.5 203.8 reduce-scatter.11
  819.7 231.0 reduce-scatter.15
  1054.6 91.9 all-gather.11
  1193.5 229.7 reduce-scatter.17
  1426.8 91.9 all-gather.13
  1565.6 229.7 reduce-scatter.19
  1799.2 91.9 all-gather.15
  1938.0 229.7 reduce-scatter.21
  2171.2 91.9 all-gather.17
  2310.0 229.9 reduce-scatter.23
  2545.9 96.3 reduce-scatter.25
  2645.6 91.4 all-gather.19
where the time goes:
time: 2770 us; the launch traced here: 2760 us
  waiting for transfers between devices  1960 us (71%)
  matrix products  401 us (14%)
  other arithmetic  235 us (8%)
  blocking collectives  82.7 us (3%)
  local copies, waits for them, and re-layouts  65.6 us (2%)
    reduce_scatter x5, waiting for transfers between devices, both_grams(): lax.psum_scatter(joined, ('dp', 'upd'), scatter_dimension=1, tiled=True)  1150 us
    all_gather x5, waiting for transfers between devices, both_grams(): lax.all_gather(lax.psum_scatter(joined, ('dp', 'upd'), scatter_dimension=...  465 us
    reduce_scatter x1, waiting for transfers between devices, local(): lax.psum_scatter(square_slope, ('dp', 'upd'), scatter_dimension=1, tiled=...  200 us
    dot_general x10, matrix products, gram_of(): jnp.einsum('wrd,wre->wde', block, block, precision=lax.Precision.HIGHEST)  98.5 us
    unnamed x16, waiting for transfers between devices  79.8 us
    all_gather x1, waiting for transfers between devices, local(): lax.all_gather(square_master.astype(jnp.bfloat16), ('dp', 'upd'), axis=1,...  67.6 us
  transfers between devices with their start and end apart: 15, of which 13 were waited for; matrix products, arithmetic and copies ran while one was open for 12% of the time, Pallas kernels for 0%

commit v1 on v0

--- a/solution.py
+++ b/solution.py
@@ -15,6 +15,18 @@
 LEARN_RATE = 0.8
 WEIGHT_DECAY = 0.01
 NEGATIVE_LARGE = -1e30
+
+
+def collect(x, axis, dim):
+    ways, here, step = (lax.axis_size(axis), lax.axis_index(axis), x.shape[dim])
+    line, have = (x, 1)
+    while have < ways:
+        line = jnp.concatenate(
+            [line, lax.ppermute(line, axis, [(d, (d - have) % ways) for d in range(ways)])],
+            axis=dim,
+        )
+        have = 2 * have
+    return jnp.roll(line, here * step, axis=dim)
 
 
 def plain_round(values):
@@ -136,13 +148,12 @@
 
 def both_grams(square, tall):
     joined = jnp.concatenate([gram_of(square), gram_of(tall)], axis=0)
-    summed = lax.all_gather(
+    summed = collect(
         lax.psum_scatter(joined, ("dp", "upd"), scatter_dimension=1, tiled=True).astype(
             jnp.bfloat16
         ),
         ("dp", "upd"),
-        axis=1,
-        tiled=True,
+        1,
     ).astype(jnp.float32)
     return (summed[:8], summed[8:])
 

time: 2770 us -> 4210 us (1.52)
  waiting for transfers between devices: 1960 us -> 3290 us
  local copies, waits for them, and re-layouts: 65.6 us -> 120 us
  other arithmetic: 235 us -> 285 us
    ppermute x0 -> x25, waiting for transfers between devices: none -> 1600 us  [collect(): lax.ppermute(line, axis, [(d, (d - have) % ways) for d in range(ways)])]
    all_gather x5 -> x0, waiting for transfers between devices: 465 us -> none  [both_grams(): lax.all_gather(lax.psum_scatter(joined, ('dp', 'upd'), scatter_dimension=...]
    unnamed x16 -> x11, waiting for transfers between devices: 79.8 us -> 269 us
    concatenate x0 -> x20, other arithmetic: none -> 54 us  [the longest x5 52.1 us: collect(): return jnp.roll(line, here * step, axis=dim)]
  transfers between devices with their start and end apart: 15 -> 35, of which waited for: 13 -> 32; matrix products, arithmetic and copies ran while one was open for 12% -> 8% of each run, Pallas kernels for 0% -> 0%
where the time goes in v1:
time: 4210 us; the launch traced here: 4200 us
  waiting for transfers between devices  3290 us (78%)
  matrix products  367 us (9%)
  other arithmetic  285 us (7%)
  local copies, waits for them, and re-layouts  120 us (3%)
  blocking collectives  82.7 us (2%)
    ppermute x25, waiting for transfers between devices, collect(): lax.ppermute(line, axis, [(d, (d - have) % ways) for d in range(ways)])  1600 us
    reduce_scatter x5, waiting for transfers between devices, both_grams(): lax.psum_scatter(joined, ('dp', 'upd'), scatter_dimension=1, tiled=True)  1160 us
    unnamed x11, waiting for transfers between devices  269 us
    reduce_scatter x1, waiting for transfers between devices, local(): lax.psum_scatter(square_slope, ('dp', 'upd'), scatter_dimension=1, tiled=...  200 us
    dot_general x10, matrix products, gram_of(): jnp.einsum('wrd,wre->wde', block, block, precision=lax.Precision.HIGHEST)  99.4 us
  transfers between devices with their start and end apart: 35, of which 32 were waited for; matrix products, arithmetic and copies ran while one was open for 8% of the time, Pallas kernels for 0%

profile of v1, /device:TPU:0, one launch (start us, length us, event | category | flops | bytes accessed | tf_op | source)
XLA Modules:
  0.0 4196.4 jit_solution(2254900155985637613)
XLA Ops:
  28.9 67.6 %all-gather.3.cloned.1.call-done = bf16[8,768,768]{2,1,0:T(8,128)(2,1)} async-done(((bf16[8,24,768]{2,1,0:T(8,128)(2,1)}), bf16[8,768,768]{2,1,0:T(8,128)(2,1)}) %all-gather.3.cloned.1.call-update) | async-done | bytes 9437200 | tf_op jit(solution)/shard_map/all_gather | solution.py:195
  225.8 35.1 fusion.191
  473.3 42.1 %psum.35 = f32[]{:T(128)} all-reduce(f32[]{:T(128)S(6)} %convert_element_type.296), channel_id=1, replica_groups=mesh['dp'=8,'upd'=4] {'dp','upd'}, use_global_device_ids=true, to_apply=%region_35.36 | all-reduce | flops 1 | bytes 8 | tf_op jit(solution)/shard_map/psum | solution.py:218
  549.2 200.4 %reduce-scatter.12.cloned.1.call-done = f32[8,24,768]{2,1,0:T(8,128)} async-done(((f32[8,768,768]{2,1,0:T(8,128)}), f32[8,24,768]{2,1,0:T(8,128)}) %reduce-scatter.12.cloned.1.call-update) | async-done | bytes 589840 | tf_op jit(solution)/shard_map/reduce_scatter | solution.py:222
  750.9 40.5 all-reduce.31
  819.8 231.1 %reduce-scatter.16.cloned.1.call-done = f32[10,24,768]{2,1,0:T(8,128)} async-done(((f32[10,768,768]{2,1,0:T(8,128)}), f32[10,24,768]{2,1,0:T(8,128)}) %reduce-scatter.16.cloned.1.call-update) | async-done | bytes 737296 | tf_op jit(solution)/shard_map/reduce_scatter | solution.py:152
  1119.8 59.2 %collective-permute-done.3 = bf16[10,192,768]{2,1,0:T(8,128)(2,1)S(1)} collective-permute-done((bf16[10,192,768]{2,1,0:T(8,128)(2,1)S(1)}, bf16[10,192,768]{2,1,0:T(8,128)(2,1)S(1)}, u32[]{:S(2)}, u32[]{:S(2)}) %collective-permute-start.3) | collective-permute-done | bytes 2949152 | tf_op jit(solution)/shard_map/ppermute | solution.py:25
  1183.1 254.6 %collective-permute-done.4 = bf16[10,384,768]{2,1,0:T(8,128)(2,1)} collective-permute-done((bf16[10,384,768]{2,1,0:T(8,128)(2,1)}, bf16[10,384,768]{2,1,0:T(8,128)(2,1)}, u32[]{:S(2)}, u32[]{:S(2)}) %collective-permute-start.4) | collective-permute-done | bytes 5898272 | tf_op jit(solution)/shard_map/ppermute | solution.py:25
  1492.4 231.8 %reduce-scatter.18.cloned.1.call-done = f32[10,24,768]{2,1,0:T(8,128)} async-done(((f32[10,768,768]{2,1,0:T(8,128)}), f32[10,24,768]{2,1,0:T(8,128)}) %reduce-scatter.18.cloned.1.call-update) | async-done | bytes 737296 | tf_op jit(solution)/shard_map/reduce_scatter | solution.py:152
  1751.0 34.8 collective-permute-done.7
  1791.4 60.3 %collective-permute-done.8 = bf16[10,192,768]{2,1,0:T(8,128)(2,1)S(1)} collective-permute-done((bf16[10,192,768]{2,1,0:T(8,128)(2,1)S(1)}, bf16[10,192,768]{2,1,0:T(8,128)(2,1)S(1)}, u32[]{:S(2)}, u32[]{:S(2)}) %collective-permute-start.8) | collective-permute-done | bytes 2949152 | tf_op jit(solution)/shard_map/ppermute | solution.py:25
  1854.4 254.4 %collective-permute-done.9 = bf16[10,384,768]{2,1,0:T(8,128)(2,1)S(1)} collective-permute-done((bf16[10,384,768]{2,1,0:T(8,128)(2,1)S(1)}, bf16[10,384,768]{2,1,0:T(8,128)(2,1)S(1)}, u32[]{:S(2)}, u32[]{:S(2)}) %collective-permute-start.9) | collective-permute-done | bytes 5898272 | tf_op jit(solution)/shard_map/ppermute | solution.py:25
  2160.8 231.7 %reduce-scatter.20.cloned.1.call-done = f32[10,24,768]{2,1,0:T(8,128)} async-done(((f32[10,768,768]{2,1,0:T(8,128)}), f32[10,24,768]{2,1,0:T(8,128)}) %reduce-scatter.20.cloned.1.call-update) | async-done | bytes 737296 | tf_op jit(solution)/shard_map/reduce_scatter | solution.py:152
  2419.5 34.7 collective-permute-done.12
  2459.7 60.2 %collective-permute-done.13 = bf16[10,192,768]{2,1,0:T(8,128)(2,1)S(1)} collective-permute-done((bf16[10,192,768]{2,1,0:T(8,128)(2,1)S(1)}, bf16[10,192,768]{2,1,0:T(8,128)(2,1)S(1)}, u32[]{:S(2)}, u32[]{:S(2)}) %collective-permute-start.13) | collective-permute-done | bytes 2949152 | tf_op jit(solution)/shard_map/ppermute | solution.py:25
  2522.7 254.4 %collective-permute-done.14 = bf16[10,384,768]{2,1,0:T(8,128)(2,1)S(1)} collective-permute-done((bf16[10,384,768]{2,1,0:T(8,128)(2,1)S(1)}, bf16[10,384,768]{2,1,0:T(8,128)(2,1)S(1)}, u32[]{:S(2)}, u32[]{:S(2)}) %collective-permute-start.14) | collective-permute-done | bytes 5898272 | tf_op jit(solution)/shard_map/ppermute | solution.py:25
  2829.1 231.9 %reduce-scatter.22.cloned.1.call-done = f32[10,24,768]{2,1,0:T(8,128)} async-done(((f32[10,768,768]{2,1,0:T(8,128)}), f32[10,24,768]{2,1,0:T(8,128)}) %reduce-scatter.22.cloned.1.call-update) | async-done | bytes 737296 | tf_op jit(solution)/shard_map/reduce_scatter | solution.py:152
  3087.7 34.8 collective-permute-done.17
  3128.1 60.3 %collective-permute-done.18 = bf16[10,192,768]{2,1,0:T(8,128)(2,1)S(1)} collective-permute-done((bf16[10,192,768]{2,1,0:T(8,128)(2,1)S(1)}, bf16[10,192,768]{2,1,0:T(8,128)(2,1)S(1)}, u32[]{:S(2)}, u32[]{:S(2)}) %collective-permute-start.18) | collective-permute-done | bytes 2949152 | tf_op jit(solution)/shard_map/ppermute | solution.py:25
  3191.1 254.4 %collective-permute-done.19 = bf16[10,384,768]{2,1,0:T(8,128)(2,1)S(1)} collective-permute-done((bf16[10,384,768]{2,1,0:T(8,128)(2,1)S(1)}, bf16[10,384,768]{2,1,0:T(8,128)(2,1)S(1)}, u32[]{:S(2)}, u32[]{:S(2)}) %collective-permute-start.19) | collective-permute-done | bytes 5898272 | tf_op jit(solution)/shard_map/ppermute | solution.py:25
  3497.5 232.0 %reduce-scatter.24.cloned.1.call-done = f32[10,24,768]{2,1,0:T(8,128)} async-done(((f32[10,768,768]{2,1,0:T(8,128)}), f32[10,24,768]{2,1,0:T(8,128)}) %reduce-scatter.24.cloned.1.call-update) | async-done | bytes 737296 | tf_op jit(solution)/shard_map/reduce_scatter | solution.py:152
  3756.9 34.8 collective-permute-done.22
  3798.3 59.2 %collective-permute-done.23 = bf16[10,192,768]{2,1,0:T(8,128)(2,1)S(1)} collective-permute-done((bf16[10,192,768]{2,1,0:T(8,128)(2,1)S(1)}, bf16[10,192,768]{2,1,0:T(8,128)(2,1)S(1)}, u32[]{:S(2)}, u32[]{:S(2)}) %collective-permute-start.23) | collective-permute-done | bytes 2949152 | tf_op jit(solution)/shard_map/ppermute | solution.py:25
  3888.5 268.4 %reduce-scatter.26.cloned.1.call-done = f32[96,3]{1,0:T(8,128)} async-done(((f32[3072,3]{1,0:T(8,128)}), f32[96,3]{1,0:T(8,128)}) %reduce-scatter.26.cloned.1.call-update) | async-done | bytes 1168
  (598 shorter events, 909.4 us)
Async XLA Ops:
  7.2 89.2 %all-gather.3.cloned.1.call-start = ((), (), s32[]{:S(2)}) async-start(), calls=%async_computation.8 | async-start | bytes 9732096 | tf_op jit(solution)/shard_map/all_gather | solution.py:195
  9.2 203.5 %all-gather.5.cloned.1.call-start = ((), (), s32[]{:S(2)}) async-start(), calls=%async_computation.9 | async-start | bytes 9732096 | tf_op jit(solution)/shard_map/all_gather | solution.py:196
  11.1 536.8 %reduce-scatter.14.cloned.1.call-start = ((), (), s32[]{:S(2)}) async-start(), calls=%async_computation.11 | async-start | bytes 19464192 | tf_op jit(solution)/shard_map/reduce_scatter | solution.py:223
  333.8 415.8 %reduce-scatter.12.cloned.1.call-start = ((), (), s32[]{:S(2)}) async-start(), calls=%async_computation.10 | async-start | bytes 19464192 | tf_op jit(solution)/shard_map/reduce_scatter | solution.py:222
  471.4 579.5 %reduce-scatter.16.cloned.1.call-start = ((), (), s32[]{:S(2)}) async-start(), calls=%async_computation.12 | async-start | bytes 24330240 | tf_op jit(solution)/shard_map/reduce_scatter | solution.py:152
  819.8 904.4 %reduce-scatter.18.cloned.1.call-start = ((), (), s32[]{:S(2)}) async-start(), calls=%async_computation.13 | async-start | bytes 24330240 | tf_op jit(solution)/shard_map/reduce_scatter | solution.py:152
  1113.5 65.5 %collective-permute-start.3 = (bf16[10,192,768]{2,1,0:T(8,128)(2,1)S(1)}, bf16[10,192,768]{2,1,0:T(8,128)(2,1)S(1)}, u32[]{:S(2)}, u32[]{:S(2)}) collective-permute-start(bf16[10,192,768]{2,1,0:T(8,128)(2,1)S(1)} %pad_maximum_fusion.5), channel_id=1, source_target_pairs={{0,24},{1,25},{2,26},{3,27},{4,28},{5,29},{6,30},{7,31},{8,0},{9,1... | collective-permute-start | bytes 8847368 | tf_op jit(solution)/shard_map/ppermute | solution.py:25
  1182.3 255.4 %collective-permute-start.4 = (bf16[10,384,768]{2,1,0:T(8,128)(2,1)}, bf16[10,384,768]{2,1,0:T(8,128)(2,1)}, u32[]{:S(2)}, u32[]{:S(2)}) collective-permute-start(bf16[10,384,768]{2,1,0:T(8,128)(2,1)} %get-tuple-element.103), channel_id=1, source_target_pairs={{0,16},{1,17},{2,18},{3,19},{4,20},{5,21},{6,22},{7,23},{8,24},{9,... | collective-permute-start | bytes 17694728 | tf_op jit(solution)/shard_map/ppermute | solution.py:25
  1492.4 900.1 %reduce-scatter.20.cloned.1.call-start = ((), (), s32[]{:S(2)}) async-start(), calls=%async_computation.14 | async-start | bytes 24330240 | tf_op jit(solution)/shard_map/reduce_scatter | solution.py:152
  1750.9 34.9 collective-permute-start.7
  1786.0 65.7 %collective-permute-start.8 = (bf16[10,192,768]{2,1,0:T(8,128)(2,1)S(1)}, bf16[10,192,768]{2,1,0:T(8,128)(2,1)S(1)}, u32[]{:S(2)}, u32[]{:S(2)}) collective-permute-start(bf16[10,192,768]{2,1,0:T(8,128)(2,1)S(1)} %pad_maximum_fusion.6), channel_id=1, source_target_pairs={{0,24},{1,25},{2,26},{3,27},{4,28},{5,29},{6,30},{7,31},{8,0},{9,1... | collective-permute-start | bytes 8847368 | tf_op jit(solution)/shard_map/ppermute | solution.py:25
  1853.7 255.0 %collective-permute-start.9 = (bf16[10,384,768]{2,1,0:T(8,128)(2,1)S(1)}, bf16[10,384,768]{2,1,0:T(8,128)(2,1)S(1)}, u32[]{:S(2)}, u32[]{:S(2)}) collective-permute-start(bf16[10,384,768]{2,1,0:T(8,128)(2,1)S(1)} %get-tuple-element.101), channel_id=1, source_target_pairs={{0,16},{1,17},{2,18},{3,19},{4,20},{5,21},{6,22},{7,23},{8,24},{9,... | collective-permute-start | bytes 17694728 | tf_op jit(solution)/shard_map/ppermute | solution.py:25
  2160.7 900.3 %reduce-scatter.22.cloned.1.call-start = ((), (), s32[]{:S(2)}) async-start(), calls=%async_computation.15 | async-start | bytes 24330240 | tf_op jit(solution)/shard_map/reduce_scatter | solution.py:152
  2419.4 34.7 collective-permute-start.12
  2454.4 65.6 %collective-permute-start.13 = (bf16[10,192,768]{2,1,0:T(8,128)(2,1)S(1)}, bf16[10,192,768]{2,1,0:T(8,128)(2,1)S(1)}, u32[]{:S(2)}, u32[]{:S(2)}) collective-permute-start(bf16[10,192,768]{2,1,0:T(8,128)(2,1)S(1)} %pad_maximum_fusion.7), channel_id=1, source_target_pairs={{0,24},{1,25},{2,26},{3,27},{4,28},{5,29},{6,30},{7,31},{8,0},{9,1... | collective-permute-start | bytes 8847368 | tf_op jit(solution)/shard_map/ppermute | solution.py:25
  2522.0 255.1 %collective-permute-start.14 = (bf16[10,384,768]{2,1,0:T(8,128)(2,1)S(1)}, bf16[10,384,768]{2,1,0:T(8,128)(2,1)S(1)}, u32[]{:S(2)}, u32[]{:S(2)}) collective-permute-start(bf16[10,384,768]{2,1,0:T(8,128)(2,1)S(1)} %get-tuple-element.99), channel_id=1, source_target_pairs={{0,16},{1,17},{2,18},{3,19},{4,20},{5,21},{6,22},{7,23},{8,24},{9,... | collective-permute-start | bytes 17694728 | tf_op jit(solution)/shard_map/ppermute | solution.py:25
  2829.0 900.5 %reduce-scatter.24.cloned.1.call-start = ((), (), s32[]{:S(2)}) async-start(), calls=%async_computation.16 | async-start | bytes 24330240 | tf_op jit(solution)/shard_map/reduce_scatter | solution.py:152
  3087.7 34.9 collective-permute-start.17
  3122.8 65.7 %collective-permute-start.18 = (bf16[10,192,768]{2,1,0:T(8,128)(2,1)S(1)}, bf16[10,192,768]{2,1,0:T(8,128)(2,1)S(1)}, u32[]{:S(2)}, u32[]{:S(2)}) collective-permute-start(bf16[10,192,768]{2,1,0:T(8,128)(2,1)S(1)} %pad_maximum_fusion.8), channel_id=1, source_target_pairs={{0,24},{1,25},{2,26},{3,27},{4,28},{5,29},{6,30},{7,31},{8,0},{9,1... | collective-permute-start | bytes 8847368 | tf_op jit(solution)/shard_map/ppermute | solution.py:25
  3190.5 255.0 %collective-permute-start.19 = (bf16[10,384,768]{2,1,0:T(8,128)(2,1)S(1)}, bf16[10,384,768]{2,1,0:T(8,128)(2,1)S(1)}, u32[]{:S(2)}, u32[]{:S(2)}) collective-permute-start(bf16[10,384,768]{2,1,0:T(8,128)(2,1)S(1)} %get-tuple-element.97), channel_id=1, source_target_pairs={{0,16},{1,17},{2,18},{3,19},{4,20},{5,21},{6,22},{7,23},{8,24},{9,... | collective-permute-start | bytes 17694728 | tf_op jit(solution)/shard_map/ppermute | solution.py:25
  3497.5 659.4 %reduce-scatter.26.cloned.1.call-start = ((), (), s32[]{:S(2)}) async-start(), calls=%async_computation.17 | async-start | bytes 1622016
  3756.8 34.9 collective-permute-start.22
  3792.0 65.6 %collective-permute-start.23 = (bf16[10,192,768]{2,1,0:T(8,128)(2,1)S(1)}, bf16[10,192,768]{2,1,0:T(8,128)(2,1)S(1)}, u32[]{:S(2)}, u32[]{:S(2)}) collective-permute-start(bf16[10,192,768]{2,1,0:T(8,128)(2,1)S(1)} %pad_maximum_fusion.9), channel_id=1, source_target_pairs={{0,24},{1,25},{2,26},{3,27},{4,28},{5,29},{6,30},{7,31},{8,0},{9,1... | collective-permute-start | bytes 8847368 | tf_op jit(solution)/shard_map/ppermute | solution.py:25
  3860.8 300.1 %collective-permute-start.24 = (bf16[10,384,768]{2,1,0:T(8,128)(2,1)}, bf16[10,384,768]{2,1,0:T(8,128)(2,1)}, u32[]{:S(2)}, u32[]{:S(2)}) collective-permute-start(bf16[10,384,768]{2,1,0:T(8,128)(2,1)} %get-tuple-element.95), channel_id=1, source_target_pairs={{0,16},{1,17},{2,18},{3,19},{4,20},{5,21},{6,22},{7,23},{8,24},{9,... | collective-permute-start | bytes 17694728 | tf_op jit(solution)/shard_map/ppermute | solution.py:25
  (148 other events, 5441.6 us)
Sparse Core Ops, SparseCore 0:
  11.5 84.8 all-gather.2
  99.9 80.6 all-gather.4
  334.0 205.2 reduce-scatter.13
  545.5 204.0 reduce-scatter.11
  819.9 230.9 reduce-scatter.15
  1492.5 231.6 reduce-scatter.17
  2160.9 231.5 reduce-scatter.19
  2829.1 231.8 reduce-scatter.21
  3497.6 231.8 reduce-scatter.23
  3867.1 289.7 reduce-scatter.25
